TPU v7x, 32 devices: a whole 2x2x4 slice. The times are simulated.
32 devices in a mesh: row: 8 (over y, x, core), col: 4 (over z).
Axes of the slice: x: 2, y: 2, z: 4, core: 2. Of those that a mesh axis runs over, the one named last changes fastest.
Arguments:
- alignment: float32 [32, 384, 64], P('col', 'row'), may hold values from -6 to 6
- pair_rep: float32 [384, 384, 128], P('row', 'col'), may hold values from -6 to 6
- seq_mask: int32 [32], P('col'), may hold values 0 or 1
- res_mask: int32 [384], P('row'), may hold values 0 or 1
- left_weight: float32 [64, 32], replicated, may hold values from -0.75 to 0.75
- right_weight: float32 [64, 32], replicated, may hold values from -0.75 to 0.75
- w_outer: float32 [1024, 128], replicated, may hold values from -4 to 4
- w_logits: float32 [128, 8], replicated, may hold values from -45 to 45
- value_weight: float32 [64, 256], replicated, may hold values from -0.75 to 0.75
- gate_weight: float32 [64, 256], replicated, may hold values from -0.75 to 0.75
- output_weight: float32 [256, 64], replicated, may hold values from -6 to 6
Outputs:
- alignment_out: float32 [32, 384, 64], P('col', 'row')
- pair_out: float32 [384, 384, 128], P('row', 'col')
All inputs are finite; a program needn't handle non-finite values. No bound on the sum of `seq_mask` or of `res_mask` on one device may be relied on, other than what follows from the above.
Results may differ from a plain program's by a relative error of at most 0.0003.
Values sent between devices are 32-bit elements; how exact they have to be, the bound alone decides.
A program may use at most 128 MiB of HBM per device.

v0:
```python
import functools

import jax
import jax.numpy as jnp
from jax import lax
from jax.experimental import pallas as pl
from jax.experimental.pallas import tpu as pltpu
from jax.sharding import PartitionSpec as P

MESH = pl.DeviceIdType.MESH
F32 = jnp.float32
BF16 = jnp.bfloat16
epsilon = 1e-05
VMEM_LIMIT = 60 * 1024 * 1024


def layer_norm(values):
    center = jnp.mean(values, axis=-1, keepdims=True)
    centred = values - center
    return centred * lax.rsqrt(jnp.mean(centred * centred, axis=-1, keepdims=True) + epsilon)


def split(values):
    high = values.astype(BF16)
    return high, (values - high.astype(F32)).astype(BF16)


def dot(left, right):
    return jnp.dot(left, right, preferred_element_type=F32)


def dot_split(left, right_high, right_low):
    high, low = split(left)
    return dot(high, right_high) + (dot(low, right_high) + dot(high, right_low))


def exchange_kernel(
    n_row,
    n_col,
    ratio,
    seq_ref,
    res_ref,
    align_ref,
    left_w_ref,
    right_w_ref,
    left_out,
    right_out,
    norm_out,
    rows_buf,
    masked_buf,
    block_buf,
    left_buf,
    right_buf,
    norm_buf,
    left_send,
    left_recv,
    right_send,
    right_recv,
    norm_send,
    norm_recv,
):
    row, col = lax.axis_index("row"), lax.axis_index("col")
    n = n_row * n_col
    me = row * n_col + col
    barrier = pltpu.get_barrier_semaphore()

    def greet(step, carry):
        other = lax.rem(me + step, n)
        pl.semaphore_signal(
            barrier,
            inc=1,
            device_id=(other // n_col, lax.rem(other, n_col)),
            device_id_type=MESH,
        )
        return carry

    lax.fori_loop(1, n, greet, 0)
    seqs, rows, width = align_ref.shape
    res_row = res_ref[...].astype(F32)
    diag = lax.broadcasted_iota(jnp.int32, (rows, rows), 0) == lax.broadcasted_iota(
        jnp.int32, (rows, rows), 1
    )
    res_col = jnp.sum(
        jnp.where(diag, jnp.broadcast_to(res_row, (rows, rows)), 0.0), axis=1, keepdims=True
    )
    lane_seq = lax.rem(lax.broadcasted_iota(jnp.int32, (width, right_w_ref.shape[1]), 1), seqs)
    seq_sum = 0.0
    for s in range(seqs):
        normed = layer_norm(align_ref[s])
        norm_buf[:, s * width : (s + 1) * width] = normed
        live = seq_ref[s].astype(F32)
        seq_sum = seq_sum + live
        masked = normed * (res_col * live)
        masked_buf[:, s * width : (s + 1) * width] = masked
        rows_buf[pl.ds(s, rows, stride=seqs), :] = masked
        block_buf[s * width : (s + 1) * width, :] = jnp.where(lane_seq == s, right_w_ref[...], 0.0)
    wl_high, wl_low = split(left_w_ref[...])
    left = dot_split(rows_buf[...], wl_high, wl_low)
    quarter = left.shape[0] // 4
    factor = left.shape[1]
    for g in range(4):
        left_buf[0:quarter, g * factor : (g + 1) * factor] = left[g * quarter : (g + 1) * quarter]
    left_buf[quarter : quarter + 8, :] = jnp.full((8, left_buf.shape[1]), seq_sum, F32)
    wr_high, wr_low = split(block_buf[...])
    right_buf[0:rows, :] = dot_split(masked_buf[...], wr_high, wr_low)
    right_buf[rows : rows + 8, 0:rows] = jnp.broadcast_to(res_row, (8, rows))
    right_buf[rows : rows + 8, rows:] = jnp.zeros((8, right_buf.shape[1] - rows), F32)

    pl.semaphore_wait(barrier, n - 1)
    dest = row // ratio
    spot = lax.rem(row, ratio)
    started = []
    for k in range(1, n_col):
        peer = lax.rem(col + k, n_col)
        copy = pltpu.make_async_remote_copy(
            left_buf,
            left_out.at[col],
            left_send.at[k],
            left_recv.at[n_col - k],
            device_id=(row, peer),
            device_id_type=MESH,
        )
        copy.start()
        started.append(copy)
    away = dest != col
    for k in range(1, n_row):
        copy = pltpu.make_async_remote_copy(
            right_buf,
            right_out.at[spot, col],
            right_send.at[k],
            right_recv.at[spot, col],
            device_id=(lax.rem(row + k, n_row), dest),
            device_id_type=MESH,
        )
        copy.start()
    own_remote = pltpu.make_async_remote_copy(
        right_buf,
        right_out.at[spot, col],
        right_send.at[0],
        right_recv.at[spot, col],
        device_id=(row, dest),
        device_id_type=MESH,
    )
    own_local = pltpu.make_async_copy(right_buf, right_out.at[spot, col], right_recv.at[spot, col])

    @pl.when(away)
    def _():
        own_remote.start()

    @pl.when(jnp.logical_not(away))
    def _():
        own_local.start()

    for k in range(1, n_row):
        peer = lax.rem(row + k, n_row)
        copy = pltpu.make_async_remote_copy(
            norm_buf,
            norm_out.at[row],
            norm_send.at[k],
            norm_recv.at[n_row - k],
            device_id=(peer, col),
            device_id_type=MESH,
        )
        copy.start()
        started.append(copy)
    left_own = pltpu.make_async_copy(left_buf, left_out.at[col], left_recv.at[0])
    left_own.start()
    norm_own = pltpu.make_async_copy(norm_buf, norm_out.at[row], norm_recv.at[0])
    norm_own.start()
    left_own.wait()
    norm_own.wait()
    for copy in started:
        copy.wait_send()
    for k in range(1, n_row):
        pltpu.make_async_copy(right_buf, right_buf, right_send.at[k]).wait()

    @pl.when(away)
    def _():
        own_remote.wait_send()

    for k in range(1, n_col):
        src = lax.rem(col + k, n_col)
        pltpu.make_async_copy(left_buf, left_out.at[src], left_recv.at[k]).wait()
    for t in range(ratio):
        for c in range(n_col):
            pltpu.make_async_copy(right_buf, right_out.at[t, c], right_recv.at[t, c]).wait()
    for k in range(1, n_row):
        src = lax.rem(row + k, n_row)
        pltpu.make_async_copy(norm_buf, norm_out.at[src], norm_recv.at[k]).wait()


def pair_kernel(
    left_ref,
    right_ref,
    outer_ref,
    logits_w_ref,
    pair_ref,
    pair_out,
    logits_out,
    w_buf,
    l_buf,
    r_buf,
    mask_buf,
    high_buf,
    low_buf,
):
    n_col = left_ref.shape[0]
    quarter = left_ref.shape[1] - 8
    ratio, rows = right_ref.shape[0], right_ref.shape[2] - 8
    k_col = right_ref.shape[3]
    factor = w_buf.shape[0] // 3
    here, cols, width = pair_ref.shape
    heads = logits_w_ref.shape[0] // 2
    seqs = k_col // factor
    step = pl.program_id(0)

    @pl.when(step == 0)
    def _():
        for b in range(factor):
            high, low = split(outer_ref[pl.ds(b, factor, stride=factor), :])
            lanes = slice(b * width, (b + 1) * width)
            w_buf[0:factor, lanes] = high
            w_buf[factor : 2 * factor, lanes] = low
            w_buf[2 * factor : 3 * factor, lanes] = high
        count = left_ref[0, quarter : quarter + 1, 0:1]
        for c in range(1, n_col):
            count = count + left_ref[c, quarter : quarter + 1, 0:1]
        scale = 1.0 / jnp.maximum(count, 1.0)
        for c in range(n_col):
            packed = left_ref[c, 0:quarter, :] * scale
            high = packed.astype(BF16).astype(F32)
            low = packed - high
            for g in range(4):
                lanes = slice(g * factor, (g + 1) * factor)
                parts = [high[:, lanes], high[:, lanes], low[:, lanes]]
                l_buf[c, g * quarter : (g + 1) * quarter, :] = jnp.concatenate(
                    parts, axis=1
                ).astype(BF16)
            for t in range(ratio):
                high_r, low_r = split(right_ref[t, c, 0:rows, :])
                lanes = slice(c * k_col, (c + 1) * k_col)
                r_buf[t * rows : (t + 1) * rows, lanes] = high_r
                r_buf[cols + t * rows : cols + (t + 1) * rows, lanes] = low_r
        for t in range(ratio):
            mask_buf[:, t * rows : (t + 1) * rows] = (
                right_ref[t, 0, rows : rows + 8, 0:rows] - 1.0
            ) * 1000000000.0

    group = here * seqs
    l_rows = jnp.concatenate(
        [l_buf[c, pl.ds(pl.multiple_of(step * group, group), group), :] for c in range(n_col)],
        axis=0,
    )
    for nb in range(factor // 2):
        mixed = dot(l_rows, w_buf[:, nb * 2 * width : (nb + 1) * 2 * width])
        tiles = jnp.concatenate(
            [
                mixed[:, :width].reshape(n_col * here, seqs, width),
                mixed[:, width:].reshape(n_col * here, seqs, width),
            ],
            axis=1,
        )
        high, low = split(tiles)
        for c in range(n_col):
            high_buf[:, c, nb] = high[c * here : (c + 1) * here]
            low_buf[:, c, nb] = low[c * here : (c + 1) * here]
    depth = n_col * k_col
    r_both = r_buf[...]
    w_both = logits_w_ref[...]
    nt = (((1,), (1,)), ((), ()))
    for p in range(here // 2):
        right_high = jnp.concatenate(
            [high_buf[2 * p + t].reshape(depth, width) for t in range(2)], axis=1
        )
        right_low = jnp.concatenate(
            [low_buf[2 * p + t].reshape(depth, width) for t in range(2)], axis=1
        )
        first = dot(r_both, right_high)
        sums = first[:cols] + (first[cols:] + dot(r_both[:cols], right_low))
        for t in range(2):
            i = 2 * p + t
            pair = pair_ref[i] + sums[:, t * width : (t + 1) * width]
            pair_out[i] = pair
            high, low = split(layer_norm(pair))
            one = lax.dot_general(w_both, high, nt, preferred_element_type=F32)
            two = lax.dot_general(w_both, low, nt, preferred_element_type=F32)
            logits = one[:heads] + (one[heads:] + two[:heads])
            logits_out[i * heads : (i + 1) * heads, :] = logits + mask_buf[...]


def average_kernel(
    n_col,
    logits_ref,
    norm_ref,
    align_ref,
    value_w_ref,
    gate_w_ref,
    output_w_ref,
    out_ref,
    slots,
    sends,
    recvs,
):
    row, col = lax.axis_index("row"), lax.axis_index("col")
    barrier = pltpu.get_barrier_semaphore()
    for k in range(1, n_col):
        pl.semaphore_signal(
            barrier, inc=1, device_id=(row, lax.rem(col + k, n_col)), device_id_type=MESH
        )
    pl.semaphore_wait(barrier, n_col - 1)
    copies = []
    for k in range(1, n_col):
        copy = pltpu.make_async_remote_copy(
            logits_ref,
            slots.at[col],
            sends.at[k],
            recvs.at[n_col - k],
            device_id=(row, lax.rem(col + k, n_col)),
            device_id_type=MESH,
        )
        copy.start()
        copies.append(copy)
    own = pltpu.make_async_copy(logits_ref, slots.at[col], recvs.at[0])
    own.start()
    seqs, rows, width = align_ref.shape
    total_rows, cols = logits_ref.shape
    heads = total_rows // rows
    channels = value_w_ref.shape[1]
    head_width = channels // heads
    wv_high, wv_low = split(value_w_ref[...])
    wg_high, wg_low = split(gate_w_ref[...])
    wo_high, wo_low = split(output_w_ref[...])
    own_head = (
        lax.broadcasted_iota(jnp.int32, (heads, channels), 1) // head_width
        == lax.broadcasted_iota(jnp.int32, (heads, channels), 0)
    ).astype(F32)
    own.wait()
    for copy in copies:
        copy.wait_send()
    for k in range(1, n_col):
        src = lax.rem(col + k, n_col)
        pltpu.make_async_copy(logits_ref, slots.at[src], recvs.at[k]).wait()
    top = jnp.max(slots[0], axis=1, keepdims=True)
    for c in range(1, n_col):
        top = jnp.maximum(top, jnp.max(slots[c], axis=1, keepdims=True))
    total = jnp.zeros_like(top)
    for c in range(n_col):
        terms = jnp.exp(slots[c] - top)
        slots[c] = terms
        total = total + jnp.sum(terms, axis=1, keepdims=True)
    inverse = 1.0 / total
    mixed = None
    for c in range(n_col):
        high, low = split(norm_ref[c * cols : (c + 1) * cols, :])
        part = dot_split(slots[c] * inverse, high, low)
        mixed = part if mixed is None else mixed + part
    for s in range(seqs):
        wide = dot_split(mixed[:, s * width : (s + 1) * width], wv_high, wv_low)
        averaged = jnp.sum(wide.reshape(rows, heads, channels) * own_head[None], axis=1)
        align = align_ref[s]
        gate = jax.nn.sigmoid(dot_split(layer_norm(align), wg_high, wg_low))
        out_ref[s] = align + dot_split(gate * averaged, wo_high, wo_low)


def per_device(
    n_row,
    n_col,
    alignment,
    pair_rep,
    seq_mask,
    res_mask,
    left_weight,
    right_weight,
    w_outer,
    w_logits,
    value_weight,
    gate_weight,
    output_weight,
):
    seqs, rows, width = alignment.shape
    cols, pair_width = pair_rep.shape[1], pair_rep.shape[2]
    factor = left_weight.shape[1]
    heads = w_logits.shape[1]
    ratio = cols // rows
    k_col = factor * seqs
    quarter = rows * seqs // 4
    vmem = pl.BlockSpec(memory_space=pltpu.VMEM)
    smem = pl.BlockSpec(memory_space=pltpu.SMEM)
    dma = pltpu.SemaphoreType.DMA
    left_shape = (quarter + 8, 4 * factor)
    right_shape = (rows + 8, k_col)
    norm_shape = (rows, seqs * width)
    left_all, right_all, norm_all = pl.pallas_call(
        functools.partial(exchange_kernel, n_row, n_col, ratio),
        out_shape=(
            jax.ShapeDtypeStruct((n_col,) + left_shape, F32),
            jax.ShapeDtypeStruct((ratio, n_col) + right_shape, F32),
            jax.ShapeDtypeStruct((n_row,) + norm_shape, F32),
        ),
        in_specs=[smem, vmem, vmem, vmem, vmem],
        out_specs=(vmem, vmem, vmem),
        scratch_shapes=[
            pltpu.VMEM((rows * seqs, width), F32),
            pltpu.VMEM(norm_shape, F32),
            pltpu.VMEM((seqs * width, k_col), F32),
            pltpu.VMEM(left_shape, F32),
            pltpu.VMEM(right_shape, F32),
            pltpu.VMEM(norm_shape, F32),
            dma((n_col,)),
            dma((n_col,)),
            dma((n_row,)),
            dma((ratio, n_col)),
            dma((n_row,)),
            dma((n_row,)),
        ],
        compiler_params=pltpu.CompilerParams(
            collective_id=0, has_side_effects=True, vmem_limit_bytes=VMEM_LIMIT
        ),
        name="exchange",
    )(
        seq_mask,
        res_mask.reshape(1, rows),
        alignment,
        left_weight,
        jnp.repeat(right_weight, seqs, axis=1),
    )
    here = 8
    wt = w_logits.T
    wt_high = wt.astype(BF16)
    wt_low = (wt - lax.reduce_precision(wt, 8, 7)).astype(BF16)
    full = lambda shape: pl.BlockSpec(shape, lambda i: (0,) * len(shape), pipeline_mode=pl.Buffered(1))
    pair_out, logits = pl.pallas_call(
        pair_kernel,
        grid=(rows // here,),
        out_shape=(
            jax.ShapeDtypeStruct(pair_rep.shape, F32),
            jax.ShapeDtypeStruct((rows * heads, cols), F32),
        ),
        in_specs=[
            full(left_all.shape),
            full(right_all.shape),
            full(w_outer.shape),
            full((2 * heads, pair_width)),
            pl.BlockSpec((here, cols, pair_width), lambda i: (i, 0, 0)),
        ],
        out_specs=(
            pl.BlockSpec((here, cols, pair_width), lambda i: (i, 0, 0)),
            pl.BlockSpec((here * heads, cols), lambda i: (i, 0)),
        ),
        scratch_shapes=[
            pltpu.VMEM((3 * factor, factor * pair_width), BF16),
            pltpu.VMEM((n_col, rows * seqs, 3 * factor), BF16),
            pltpu.VMEM((2 * cols, n_col * k_col), BF16),
            pltpu.VMEM((8, cols), F32),
            pltpu.VMEM((here, n_col, factor // 2, 2 * seqs, pair_width), BF16),
            pltpu.VMEM((here, n_col, factor // 2, 2 * seqs, pair_width), BF16),
        ],
        compiler_params=pltpu.CompilerParams(vmem_limit_bytes=VMEM_LIMIT),
        name="pair",
    )(left_all, right_all, w_outer, jnp.concatenate([wt_high, wt_low], axis=0), pair_rep)
    alignment_out = pl.pallas_call(
        functools.partial(average_kernel, n_col),
        out_shape=jax.ShapeDtypeStruct(alignment.shape, F32),
        in_specs=[vmem] * 6,
        out_specs=vmem,
        scratch_shapes=[
            pltpu.VMEM((n_col,) + logits.shape, F32),
            dma((n_col,)),
            dma((n_col,)),
        ],
        compiler_params=pltpu.CompilerParams(
            collective_id=1, has_side_effects=True, vmem_limit_bytes=VMEM_LIMIT
        ),
        name="average",
    )(
        logits,
        norm_all.reshape(n_row * rows, seqs * width),
        alignment,
        value_weight,
        gate_weight,
        output_weight,
    )
    return (alignment_out, pair_out)


def solution(mesh):
    in_specs = (P("col", "row", None), P("row", "col", None), P("col"), P("row")) + (P(),) * 7
    out_specs = (P("col", "row", None), P("row", "col", None))
    return jax.shard_map(
        functools.partial(per_device, mesh.shape["row"], mesh.shape["col"]),
        mesh=mesh,
        in_specs=in_specs,
        out_specs=out_specs,
        check_vma=False,
    )
```

profile of v0, /device:TPU:0, one launch (start us, length us, event | category | flops | bytes accessed | tf_op | source)
XLA Modules:
  0.0 101.9 jit_solution(14538874913763589846)
XLA Ops:
  0.6 0.0 copy-start
  0.6 0.0 copy-start.1
  0.7 0.7 copy-done
  1.4 0.7 copy.17.right_w_ref
  2.1 1.4 %copy.16.left_w_ref = f32[64,32]{1,0:T(8,128)} copy(f32[64,32]{0,1:T(8,128)} %param.15) | data formatting | bytes 16384 | tf_op args[4]
  3.5 44.1 %exchange.1 = (f32[4,104,128]{2,1,0:T(8,128)}, f32[2,4,56,256]{3,2,1,0:T(8,128)}, f32[8,48,512]{2,1,0:T(8,128)}) custom-call(s32[8]{0:T(128)} %seq_ref.1, s32[1,48]{1,0:T(1,128)} %bitcast.8, f32[8,48,64]{2,1,0:T(8,128)} %align_ref.3, f32[64,32]{1,0:T(8,128)} %copy.16.left_w_ref, f32[64,256]{1,0:T(8,128)} %copy.17.right_w_ref), custom_call_target="tpu_custom_call" | custom-call | tf_op jit(solution)/shard_map/exchange/pallas_call | solution.py:393
  47.6 0.7 bitcast_convert_fusion
  48.3 0.7 fusion
  49.0 0.6 pad_maximum_fusion.logits_w_ref
  49.6 25.3 %pair.1 = (f32[48,96,128]{2,1,0:T(8,128)}, f32[384,96]{1,0:T(8,128)}) custom-call(f32[4,104,128]{2,1,0:T(8,128)} %get-tuple-element.7.left_ref, f32[2,4,56,256]{3,2,1,0:T(8,128)} %get-tuple-element.8.right_ref, f32[1024,128]{1,0:T(8,128)} %outer_ref.1, bf16[16,128]{1,0:T(8,128)(2,1)} %pad_maximum_fusion.logits_w_ref, f32[48,96,128]{2,1,0:T(8,128)} %pair_ref.1), custom_call_target="tpu_custom_call" | custom-call | tf_op jit(solution)/shard_map/pair/pallas_call | solution.py:432
  74.9 0.0 copy-done.1
  74.9 0.7 copy.18.output_w_ref
  75.7 24.6 %average.1 = f32[8,48,64]{2,1,0:T(8,128)} custom-call(f32[384,96]{1,0:T(8,128)} %get-tuple-element.9.logits_ref, f32[384,512]{1,0:T(8,128)} %bitcast.7, f32[8,48,64]{2,1,0:T(8,128)} %align_ref.3, f32[64,256]{1,0:T(8,128)} %value_w_ref.1, f32[64,256]{1,0:T(8,128)} %gate_w_ref.1, f32[256,64]{1,0:T(8,128)} %copy.18.output_w_ref), custom_call_target="tpu_custom_call" | custom-call | tf_op jit(solution)/shard_map/average/pallas_call | solution.py:461
  100.3 1.6 %copy.20 = f32[8,48,64]{2,1,0:T(8,128)} copy(f32[8,48,64]{2,1,0:T(8,128)} %average.1) | data formatting | bytes 196608
  (1 shorter events, 0.0 us)
Async XLA Ops:
  0.6 0.7 copy-start
  0.6 74.3 %copy-start.1 = (f32[256,64]{0,1:T(8,128)S(1)}, f32[256,64]{0,1:T(8,128)}, u32[]{:S(2)}) copy-start(f32[256,64]{0,1:T(8,128)} %param.21) | copy-start | bytes 196612
where the time goes:
time: 103 us; the launch traced here: 102 us
  Pallas kernels  94.1 us (91%)
  local copies, waits for them, and re-layouts  5.21 us (5%)
  other arithmetic  1.97 us (2%)
    pallas_call x1, Pallas kernels, per_device(): pl.pallas_call(functools.partial(exchange_kernel, n_row, n_col, ratio), o...  44.1 us
    pallas_call x1, Pallas kernels, per_device(): pl.pallas_call(pair_kernel, grid=(rows // here,), out_shape=(jax.ShapeDty...  25.3 us
    pallas_call x1, Pallas kernels, per_device(): pl.pallas_call(functools.partial(average_kernel, n_col), out_shape=jax.Sh...  24.6 us
    unnamed x7, local copies, waits for them, and re-layouts  4.49 us

commit v1 on v0

--- a/solution.py
+++ b/solution.py
@@ -29,9 +29,13 @@
     return jnp.dot(left, right, preferred_element_type=F32)
 
 
-def dot_split(left, right_high, right_low):
+def dot_t(left, right):
+    return lax.dot_general(left, right, (((1,), (1,)), ((), ())), preferred_element_type=F32)
+
+
+def dot_split(left, right_high, right_low, multiply=dot):
     high, low = split(left)
-    return dot(high, right_high) + (dot(low, right_high) + dot(high, right_low))
+    return multiply(high, right_high) + (multiply(low, right_high) + multiply(high, right_low))
 
 
 def exchange_kernel(
@@ -45,19 +49,16 @@
     right_w_ref,
     left_out,
     right_out,
-    norm_out,
+    norm_buf,
     rows_buf,
     masked_buf,
     block_buf,
     left_buf,
     right_buf,
-    norm_buf,
     left_send,
     left_recv,
     right_send,
     right_recv,
-    norm_send,
-    norm_recv,
 ):
     row, col = lax.axis_index("row"), lax.axis_index("col")
     n = n_row * n_col
@@ -83,7 +84,9 @@
     res_col = jnp.sum(
         jnp.where(diag, jnp.broadcast_to(res_row, (rows, rows)), 0.0), axis=1, keepdims=True
     )
-    lane_seq = lax.rem(lax.broadcasted_iota(jnp.int32, (width, right_w_ref.shape[1]), 1), seqs)
+    factor = right_w_ref.shape[0]
+    spread = jnp.broadcast_to(right_w_ref[...][:, None, :], (factor, seqs, width))
+    row_seq = lax.broadcasted_iota(jnp.int32, (factor, seqs, width), 1)
     seq_sum = 0.0
     for s in range(seqs):
         normed = layer_norm(align_ref[s])
@@ -93,16 +96,17 @@
         masked = normed * (res_col * live)
         masked_buf[:, s * width : (s + 1) * width] = masked
         rows_buf[pl.ds(s, rows, stride=seqs), :] = masked
-        block_buf[s * width : (s + 1) * width, :] = jnp.where(lane_seq == s, right_w_ref[...], 0.0)
+        block_buf[:, s * width : (s + 1) * width] = jnp.where(row_seq == s, spread, 0.0).reshape(
+            factor * seqs, width
+        )
     wl_high, wl_low = split(left_w_ref[...])
-    left = dot_split(rows_buf[...], wl_high, wl_low)
+    left = dot_split(rows_buf[...], wl_high, wl_low, dot_t)
     quarter = left.shape[0] // 4
-    factor = left.shape[1]
     for g in range(4):
         left_buf[0:quarter, g * factor : (g + 1) * factor] = left[g * quarter : (g + 1) * quarter]
     left_buf[quarter : quarter + 8, :] = jnp.full((8, left_buf.shape[1]), seq_sum, F32)
     wr_high, wr_low = split(block_buf[...])
-    right_buf[0:rows, :] = dot_split(masked_buf[...], wr_high, wr_low)
+    right_buf[0:rows, :] = dot_split(masked_buf[...], wr_high, wr_low, dot_t)
     right_buf[rows : rows + 8, 0:rows] = jnp.broadcast_to(res_row, (8, rows))
     right_buf[rows : rows + 8, rows:] = jnp.zeros((8, right_buf.shape[1] - rows), F32)
 
@@ -151,24 +155,9 @@
     def _():
         own_local.start()
 
-    for k in range(1, n_row):
-        peer = lax.rem(row + k, n_row)
-        copy = pltpu.make_async_remote_copy(
-            norm_buf,
-            norm_out.at[row],
-            norm_send.at[k],
-            norm_recv.at[n_row - k],
-            device_id=(peer, col),
-            device_id_type=MESH,
-        )
-        copy.start()
-        started.append(copy)
     left_own = pltpu.make_async_copy(left_buf, left_out.at[col], left_recv.at[0])
     left_own.start()
-    norm_own = pltpu.make_async_copy(norm_buf, norm_out.at[row], norm_recv.at[0])
-    norm_own.start()
     left_own.wait()
-    norm_own.wait()
     for copy in started:
         copy.wait_send()
     for k in range(1, n_row):
@@ -184,38 +173,102 @@
     for t in range(ratio):
         for c in range(n_col):
             pltpu.make_async_copy(right_buf, right_out.at[t, c], right_recv.at[t, c]).wait()
-    for k in range(1, n_row):
-        src = lax.rem(row + k, n_row)
-        pltpu.make_async_copy(norm_buf, norm_out.at[src], norm_recv.at[k]).wait()
 
 
 def pair_kernel(
+    n_row,
+    n_col,
     left_ref,
     right_ref,
     outer_ref,
     logits_w_ref,
+    norm_ref,
     pair_ref,
     pair_out,
-    logits_out,
+    slots,
+    norm_out,
     w_buf,
     l_buf,
     r_buf,
     mask_buf,
     high_buf,
     low_buf,
+    logits_buf,
+    logits_send,
+    logits_recv,
+    logits_own,
+    norm_send,
+    norm_recv,
+    relay_send,
+    relay_recv,
+    norm_local,
 ):
-    n_col = left_ref.shape[0]
+    row, col = lax.axis_index("row"), lax.axis_index("col")
+    half = n_row // 2
+    chip, core = row // 2, lax.rem(row, 2)
+    partner = 2 * chip + 1 - core
+    barrier = pltpu.get_barrier_semaphore()
     quarter = left_ref.shape[1] - 8
     ratio, rows = right_ref.shape[0], right_ref.shape[2] - 8
     k_col = right_ref.shape[3]
     factor = w_buf.shape[0] // 3
     here, cols, width = pair_ref.shape
-    heads = logits_w_ref.shape[0] // 2
+    heads = logits_w_ref.shape[0]
     seqs = k_col // factor
     step = pl.program_id(0)
+    steps = pl.num_programs(0)
+
+    def peer_row(k):
+        return 2 * lax.rem(chip + k, half) + core
+
+    def norm_copy(k):
+        return pltpu.make_async_remote_copy(
+            norm_ref,
+            norm_out.at[row],
+            norm_send.at[k],
+            norm_recv.at[half - k],
+            device_id=(peer_row(k), col),
+            device_id_type=MESH,
+        )
+
+    def relay_copy(k):
+        return pltpu.make_async_remote_copy(
+            norm_ref if k == 0 else norm_out.at[peer_row(k)],
+            norm_out.at[peer_row(k)],
+            relay_send.at[k],
+            relay_recv.at[k],
+            device_id=(partner, col),
+            device_id_type=MESH,
+        )
+
+    own_norm = pltpu.make_async_copy(norm_ref, norm_out.at[row], norm_local)
+    size = pair_ref.shape[0] * heads
+
+    def logits_copy(k, at):
+        part = pl.ds(pl.multiple_of(at * size, size), size)
+        return pltpu.make_async_remote_copy(
+            logits_buf.at[part],
+            slots.at[col, part],
+            logits_send.at[k, at],
+            logits_recv.at[n_col - k, at],
+            device_id=(row, lax.rem(col + k, n_col)),
+            device_id_type=MESH,
+        )
+
+    def own_logits(at):
+        part = pl.ds(pl.multiple_of(at * size, size), size)
+        return pltpu.make_async_copy(logits_buf.at[part], slots.at[col, part], logits_own.at[at])
 
     @pl.when(step == 0)
     def _():
+        for k in range(1, n_col):
+            pl.semaphore_signal(
+                barrier, inc=1, device_id=(row, lax.rem(col + k, n_col)), device_id_type=MESH
+            )
+        for k in range(1, half):
+            pl.semaphore_signal(barrier, inc=1, device_id=(peer_row(k), col), device_id_type=MESH)
+        pl.semaphore_signal(barrier, inc=1, device_id=(partner, col), device_id_type=MESH)
+        own_norm.start()
         for b in range(factor):
             high, low = split(outer_ref[pl.ds(b, factor, stride=factor), :])
             lanes = slice(b * width, (b + 1) * width)
@@ -266,8 +319,8 @@
             low_buf[:, c, nb] = low[c * here : (c + 1) * here]
     depth = n_col * k_col
     r_both = r_buf[...]
-    w_both = logits_w_ref[...]
-    nt = (((1,), (1,)), ((), ()))
+    w_high, w_low = split(logits_w_ref[...])
+    w_both = jnp.concatenate([w_high.astype(F32), w_low.astype(F32)], axis=0).astype(BF16)
     for p in range(here // 2):
         right_high = jnp.concatenate(
             [high_buf[2 * p + t].reshape(depth, width) for t in range(2)], axis=1
@@ -282,48 +335,65 @@
             pair = pair_ref[i] + sums[:, t * width : (t + 1) * width]
             pair_out[i] = pair
             high, low = split(layer_norm(pair))
-            one = lax.dot_general(w_both, high, nt, preferred_element_type=F32)
-            two = lax.dot_general(w_both, low, nt, preferred_element_type=F32)
+            one = dot_t(w_both, high)
+            two = dot_t(w_both, low)
             logits = one[:heads] + (one[heads:] + two[:heads])
-            logits_out[i * heads : (i + 1) * heads, :] = logits + mask_buf[...]
+            start = pl.multiple_of(step * size + i * heads, heads)
+            logits_buf[pl.ds(start, heads), :] = logits + mask_buf[...]
+
+    @pl.when(step == 0)
+    def _():
+        pl.semaphore_wait(barrier, n_col - 1 + half)
+        relay_copy(0).start()
+        for k in range(1, half):
+            norm_copy(k).start()
+
+    for k in range(1, n_col):
+        logits_copy(k, step).start()
+    own_logits(step).start()
+
+    @pl.when(step == steps // 2)
+    def _():
+        for k in range(1, half):
+            pltpu.make_async_copy(norm_ref, norm_out.at[peer_row(k)], norm_recv.at[k]).wait()
+            relay_copy(k).start()
+
+    @pl.when(step == steps - 1)
+    def _():
+        own_norm.wait()
+        for k in range(half):
+            other = 2 * lax.rem(chip + k, half) + 1 - core
+            relay_copy(k).wait_send()
+            pltpu.make_async_copy(norm_ref, norm_out.at[other], relay_recv.at[k]).wait()
+        for k in range(1, half):
+            norm_copy(k).wait_send()
+
+        def drain(at, carry):
+            own_logits(at).wait()
+            part = pl.ds(pl.multiple_of(at * size, size), size)
+            for k in range(1, n_col):
+                logits_copy(k, at).wait_send()
+                src = lax.rem(col + k, n_col)
+                pltpu.make_async_copy(
+                    logits_buf.at[part], slots.at[src, part], logits_recv.at[k, at]
+                ).wait()
+            return carry
+
+        lax.fori_loop(0, steps, drain, 0)
 
 
 def average_kernel(
-    n_col,
-    logits_ref,
+    slots,
     norm_ref,
     align_ref,
     value_w_ref,
     gate_w_ref,
     output_w_ref,
     out_ref,
-    slots,
-    sends,
-    recvs,
+    terms_buf,
 ):
-    row, col = lax.axis_index("row"), lax.axis_index("col")
-    barrier = pltpu.get_barrier_semaphore()
-    for k in range(1, n_col):
-        pl.semaphore_signal(
-            barrier, inc=1, device_id=(row, lax.rem(col + k, n_col)), device_id_type=MESH
-        )
-    pl.semaphore_wait(barrier, n_col - 1)
-    copies = []
-    for k in range(1, n_col):
-        copy = pltpu.make_async_remote_copy(
-            logits_ref,
-            slots.at[col],
-            sends.at[k],
-            recvs.at[n_col - k],
-            device_id=(row, lax.rem(col + k, n_col)),
-            device_id_type=MESH,
-        )
-        copy.start()
-        copies.append(copy)
-    own = pltpu.make_async_copy(logits_ref, slots.at[col], recvs.at[0])
-    own.start()
     seqs, rows, width = align_ref.shape
-    total_rows, cols = logits_ref.shape
+    n_col, total_rows, cols = slots.shape
     heads = total_rows // rows
     channels = value_w_ref.shape[1]
     head_width = channels // heads
@@ -334,32 +404,26 @@
         lax.broadcasted_iota(jnp.int32, (heads, channels), 1) // head_width
         == lax.broadcasted_iota(jnp.int32, (heads, channels), 0)
     ).astype(F32)
-    own.wait()
-    for copy in copies:
-        copy.wait_send()
-    for k in range(1, n_col):
-        src = lax.rem(col + k, n_col)
-        pltpu.make_async_copy(logits_ref, slots.at[src], recvs.at[k]).wait()
     top = jnp.max(slots[0], axis=1, keepdims=True)
     for c in range(1, n_col):
         top = jnp.maximum(top, jnp.max(slots[c], axis=1, keepdims=True))
     total = jnp.zeros_like(top)
     for c in range(n_col):
         terms = jnp.exp(slots[c] - top)
-        slots[c] = terms
+        terms_buf[c] = terms
         total = total + jnp.sum(terms, axis=1, keepdims=True)
     inverse = 1.0 / total
     mixed = None
     for c in range(n_col):
         high, low = split(norm_ref[c * cols : (c + 1) * cols, :])
-        part = dot_split(slots[c] * inverse, high, low)
+        part = dot_split(terms_buf[c] * inverse, high, low)
         mixed = part if mixed is None else mixed + part
     for s in range(seqs):
         wide = dot_split(mixed[:, s * width : (s + 1) * width], wv_high, wv_low)
         averaged = jnp.sum(wide.reshape(rows, heads, channels) * own_head[None], axis=1)
         align = align_ref[s]
         gate = jax.nn.sigmoid(dot_split(layer_norm(align), wg_high, wg_low))
-        out_ref[s] = align + dot_split(gate * averaged, wo_high, wo_low)
+        out_ref[s] = align + dot_split(gate * averaged, wo_high, wo_low, dot_t)
 
 
 def per_device(
@@ -390,28 +454,25 @@
     left_shape = (quarter + 8, 4 * factor)
     right_shape = (rows + 8, k_col)
     norm_shape = (rows, seqs * width)
-    left_all, right_all, norm_all = pl.pallas_call(
+    left_all, right_all, norm_own = pl.pallas_call(
         functools.partial(exchange_kernel, n_row, n_col, ratio),
         out_shape=(
             jax.ShapeDtypeStruct((n_col,) + left_shape, F32),
             jax.ShapeDtypeStruct((ratio, n_col) + right_shape, F32),
-            jax.ShapeDtypeStruct((n_row,) + norm_shape, F32),
+            jax.ShapeDtypeStruct(norm_shape, F32),
         ),
         in_specs=[smem, vmem, vmem, vmem, vmem],
         out_specs=(vmem, vmem, vmem),
         scratch_shapes=[
             pltpu.VMEM((rows * seqs, width), F32),
             pltpu.VMEM(norm_shape, F32),
-            pltpu.VMEM((seqs * width, k_col), F32),
+            pltpu.VMEM((k_col, seqs * width), F32),
             pltpu.VMEM(left_shape, F32),
             pltpu.VMEM(right_shape, F32),
-            pltpu.VMEM(norm_shape, F32),
             dma((n_col,)),
             dma((n_col,)),
             dma((n_row,)),
             dma((ratio, n_col)),
-            dma((n_row,)),
-            dma((n_row,)),
         ],
         compiler_params=pltpu.CompilerParams(
             collective_id=0, has_side_effects=True, vmem_limit_bytes=VMEM_LIMIT
@@ -421,31 +482,34 @@
         seq_mask,
         res_mask.reshape(1, rows),
         alignment,
-        left_weight,
-        jnp.repeat(right_weight, seqs, axis=1),
+        left_weight.T,
+        right_weight.T,
     )
     here = 8
-    wt = w_logits.T
-    wt_high = wt.astype(BF16)
-    wt_low = (wt - lax.reduce_precision(wt, 8, 7)).astype(BF16)
+    steps = rows // here
+    half = n_row // 2
+    anywhere = pl.BlockSpec(memory_space=pl.ANY)
     full = lambda shape: pl.BlockSpec(shape, lambda i: (0,) * len(shape), pipeline_mode=pl.Buffered(1))
-    pair_out, logits = pl.pallas_call(
-        pair_kernel,
-        grid=(rows // here,),
+    pair_out, slots, norm_all = pl.pallas_call(
+        functools.partial(pair_kernel, n_row, n_col),
+        grid=(steps,),
         out_shape=(
             jax.ShapeDtypeStruct(pair_rep.shape, F32),
-            jax.ShapeDtypeStruct((rows * heads, cols), F32),
+            jax.ShapeDtypeStruct((n_col, rows * heads, cols), F32),
+            jax.ShapeDtypeStruct((n_row,) + norm_shape, F32),
         ),
         in_specs=[
             full(left_all.shape),
             full(right_all.shape),
             full(w_outer.shape),
-            full((2 * heads, pair_width)),
+            full((heads, pair_width)),
+            anywhere,
             pl.BlockSpec((here, cols, pair_width), lambda i: (i, 0, 0)),
         ],
         out_specs=(
             pl.BlockSpec((here, cols, pair_width), lambda i: (i, 0, 0)),
-            pl.BlockSpec((here * heads, cols), lambda i: (i, 0)),
+            anywhere,
+            anywhere,
         ),
         scratch_shapes=[
             pltpu.VMEM((3 * factor, factor * pair_width), BF16),
@@ -454,31 +518,36 @@
             pltpu.VMEM((8, cols), F32),
             pltpu.VMEM((here, n_col, factor // 2, 2 * seqs, pair_width), BF16),
             pltpu.VMEM((here, n_col, factor // 2, 2 * seqs, pair_width), BF16),
-        ],
-        compiler_params=pltpu.CompilerParams(vmem_limit_bytes=VMEM_LIMIT),
-        name="pair",
-    )(left_all, right_all, w_outer, jnp.concatenate([wt_high, wt_low], axis=0), pair_rep)
-    alignment_out = pl.pallas_call(
-        functools.partial(average_kernel, n_col),
-        out_shape=jax.ShapeDtypeStruct(alignment.shape, F32),
-        in_specs=[vmem] * 6,
-        out_specs=vmem,
-        scratch_shapes=[
-            pltpu.VMEM((n_col,) + logits.shape, F32),
-            dma((n_col,)),
-            dma((n_col,)),
+            pltpu.VMEM((rows * heads, cols), F32),
+            dma((n_col, steps)),
+            dma((n_col, steps)),
+            dma((steps,)),
+            dma((half,)),
+            dma((half,)),
+            dma((half,)),
+            dma((half,)),
+            dma,
         ],
         compiler_params=pltpu.CompilerParams(
             collective_id=1, has_side_effects=True, vmem_limit_bytes=VMEM_LIMIT
         ),
+        name="pair",
+    )(left_all, right_all, w_outer, w_logits.T, norm_own, pair_rep)
+    alignment_out = pl.pallas_call(
+        average_kernel,
+        out_shape=jax.ShapeDtypeStruct(alignment.shape, F32),
+        in_specs=[vmem] * 6,
+        out_specs=vmem,
+        scratch_shapes=[pltpu.VMEM(slots.shape, F32)],
+        compiler_params=pltpu.CompilerParams(vmem_limit_bytes=VMEM_LIMIT),
         name="average",
     )(
-        logits,
+        slots,
         norm_all.reshape(n_row * rows, seqs * width),
         alignment,
         value_weight,
         gate_weight,
-        output_weight,
+        output_weight.T,
     )
     return (alignment_out, pair_out)
 

time: 103 us -> 84.2 us (0.82)
  Pallas kernels: 94.1 us -> 80.1 us
  local copies, waits for them, and re-layouts: 5.21 us -> 3.22 us
  other arithmetic: 1.97 us -> 0 us
    pallas_call x2, Pallas kernels: 49.9 us -> 36.4 us  [the longest x1 28.8 us: per_device(): pl.pallas_call(functools.partial(pair_kernel, n_row, n_col), grid=(steps,...]
    convert_element_type x2 -> x0, other arithmetic: 1.38 us -> none  [the longest x1 0.69 us: per_device(): wt_high = wt.astype(BF16)]
    unnamed x7 -> x1, local copies, waits for them, and re-layouts: 4.49 us -> 3.22 us
where the time goes in v1:
time: 84.2 us; the launch traced here: 84 us
  Pallas kernels  80.1 us (95%)
  local copies, waits for them, and re-layouts  3.22 us (4%)
    pallas_call x1, Pallas kernels, per_device(): pl.pallas_call(functools.partial(exchange_kernel, n_row, n_col, ratio), o...  43.7 us
    pallas_call x1, Pallas kernels, per_device(): pl.pallas_call(functools.partial(pair_kernel, n_row, n_col), grid=(steps,...  28.8 us
    pallas_call x1, Pallas kernels, per_device(): pl.pallas_call(average_kernel, out_shape=jax.ShapeDtypeStruct(alignment.s...  7.57 us
    unnamed x1, local copies, waits for them, and re-layouts  3.22 us

profile of v1, /device:TPU:0, one launch (start us, length us, event | category | flops | bytes accessed | tf_op | source)
XLA Modules:
  0.0 84.0 jit_solution(313193526390341073)
XLA Ops:
  0.6 43.7 %exchange.1 = (f32[4,104,128]{2,1,0:T(8,128)}, f32[2,4,56,256]{3,2,1,0:T(8,128)}, f32[48,512]{1,0:T(8,128)}) custom-call(s32[8]{0:T(128)} %seq_ref.1, s32[1,48]{1,0:T(1,128)} %bitcast.11, f32[8,48,64]{2,1,0:T(8,128)} %align_ref.3, f32[32,64]{1,0:T(8,128)} %bitcast.8, f32[32,64]{1,0:T(8,128)} %bitcast.9), custom_call_target="tpu_custom_call" | custom-call | tf_op jit(solution)/shard_map/exchange/pallas_call | solution.py:457
  44.3 28.8 %pair.1 = (f32[48,96,128]{2,1,0:T(8,128)}, f32[4,384,96]{2,1,0:T(8,128)}, f32[8,48,512]{2,1,0:T(8,128)}) custom-call(f32[4,104,128]{2,1,0:T(8,128)} %get-tuple-element.8.left_ref, f32[2,4,56,256]{3,2,1,0:T(8,128)} %get-tuple-element.9.right_ref, f32[1024,128]{1,0:T(8,128)} %outer_ref.1, f32[8,128]{1,0:T(8,128)} %bitcast.10, ...), custom_call_target="tpu_custom_call" | custom-call | tf_op jit(solution)/shard_map/pair/pallas_call | solution.py:493
  73.2 7.6 %average.1 = f32[8,48,64]{2,1,0:T(8,128)} custom-call(f32[4,384,96]{2,1,0:T(8,128)} %get-tuple-element.11.slots, f32[384,512]{1,0:T(8,128)} %bitcast.6, f32[8,48,64]{2,1,0:T(8,128)} %align_ref.3, f32[64,256]{1,0:T(8,128)} %value_w_ref.1, f32[64,256]{1,0:T(8,128)} %gate_w_ref.1, f32[64,256]{1,0:T(8,128)} %bitcast.7), custom_call_target="tpu_custom_call" | custom-call | tf_op jit(solution)/shard_map/average/pallas_call | solution.py:536
  80.7 3.2 %copy.14 = f32[48,96,128]{2,1,0:T(8,128)} copy(f32[48,96,128]{2,1,0:T(8,128)} %get-tuple-element.17) | data formatting | bytes 4718592

commit v2 on v1

--- a/solution.py
+++ b/solution.py
@@ -57,8 +57,11 @@
     right_buf,
     left_send,
     left_recv,
+    turn_sem,
     right_send,
     right_recv,
+    relay_send,
+    relay_recv,
 ):
     row, col = lax.axis_index("row"), lax.axis_index("col")
     n = n_row * n_col
@@ -112,67 +115,86 @@
 
     pl.semaphore_wait(barrier, n - 1)
     dest = row // ratio
-    spot = lax.rem(row, ratio)
+    spot = col * ratio + lax.rem(row, ratio)
+    away = dest != col
+    half = n_row // 2
+    chip, core = row // 2, lax.rem(row, 2)
+    partner = 2 * chip + 1 - core
+
+    def peer_row(k):
+        return 2 * lax.rem(chip + k, half) + core
+
+    turn = pltpu.make_async_remote_copy(
+        right_buf,
+        right_out.at[spot],
+        turn_sem.at[0],
+        turn_sem.at[1],
+        device_id=(spot, dest),
+        device_id_type=MESH,
+    )
+    stay = pltpu.make_async_copy(right_buf, right_out.at[spot], turn_sem.at[1])
+
+    @pl.when(away)
+    def _():
+        turn.start()
+
+    @pl.when(jnp.logical_not(away))
+    def _():
+        stay.start()
+
     started = []
     for k in range(1, n_col):
-        peer = lax.rem(col + k, n_col)
         copy = pltpu.make_async_remote_copy(
             left_buf,
             left_out.at[col],
             left_send.at[k],
             left_recv.at[n_col - k],
-            device_id=(row, peer),
+            device_id=(row, lax.rem(col + k, n_col)),
             device_id_type=MESH,
         )
         copy.start()
         started.append(copy)
-    away = dest != col
-    for k in range(1, n_row):
-        copy = pltpu.make_async_remote_copy(
-            right_buf,
-            right_out.at[spot, col],
-            right_send.at[k],
-            right_recv.at[spot, col],
-            device_id=(lax.rem(row + k, n_row), dest),
-            device_id_type=MESH,
-        )
-        copy.start()
-    own_remote = pltpu.make_async_remote_copy(
-        right_buf,
-        right_out.at[spot, col],
-        right_send.at[0],
-        right_recv.at[spot, col],
-        device_id=(row, dest),
-        device_id_type=MESH,
-    )
-    own_local = pltpu.make_async_copy(right_buf, right_out.at[spot, col], right_recv.at[spot, col])
-
-    @pl.when(away)
-    def _():
-        own_remote.start()
-
-    @pl.when(jnp.logical_not(away))
-    def _():
-        own_local.start()
-
     left_own = pltpu.make_async_copy(left_buf, left_out.at[col], left_recv.at[0])
     left_own.start()
+    pltpu.make_async_copy(right_buf, right_out.at[row], turn_sem.at[1]).wait()
+    for k in range(1, half):
+        copy = pltpu.make_async_remote_copy(
+            right_out.at[row],
+            right_out.at[row],
+            right_send.at[k],
+            right_recv.at[half - k],
+            device_id=(peer_row(k), col),
+            device_id_type=MESH,
+        )
+        copy.start()
+        started.append(copy)
+    for k in range(half):
+        src = peer_row(k)
+        if k > 0:
+            pltpu.make_async_copy(right_buf, right_out.at[src], right_recv.at[k]).wait()
+        copy = pltpu.make_async_remote_copy(
+            right_out.at[src],
+            right_out.at[src],
+            relay_send.at[k],
+            relay_recv.at[k],
+            device_id=(partner, col),
+            device_id_type=MESH,
+        )
+        copy.start()
+        started.append(copy)
     left_own.wait()
-    for copy in started:
-        copy.wait_send()
-    for k in range(1, n_row):
-        pltpu.make_async_copy(right_buf, right_buf, right_send.at[k]).wait()
-
-    @pl.when(away)
-    def _():
-        own_remote.wait_send()
-
     for k in range(1, n_col):
         src = lax.rem(col + k, n_col)
         pltpu.make_async_copy(left_buf, left_out.at[src], left_recv.at[k]).wait()
-    for t in range(ratio):
-        for c in range(n_col):
-            pltpu.make_async_copy(right_buf, right_out.at[t, c], right_recv.at[t, c]).wait()
+    for k in range(half):
+        src = 2 * lax.rem(chip + k, half) + 1 - core
+        pltpu.make_async_copy(right_buf, right_out.at[src], relay_recv.at[k]).wait()
+    for copy in started:
+        copy.wait_send()
+
+    @pl.when(away)
+    def _():
+        turn.wait_send()
 
 
 def pair_kernel(
@@ -209,8 +231,8 @@
     partner = 2 * chip + 1 - core
     barrier = pltpu.get_barrier_semaphore()
     quarter = left_ref.shape[1] - 8
-    ratio, rows = right_ref.shape[0], right_ref.shape[2] - 8
-    k_col = right_ref.shape[3]
+    ratio, rows = n_row // n_col, right_ref.shape[1] - 8
+    k_col = right_ref.shape[2]
     factor = w_buf.shape[0] // 3
     here, cols, width = pair_ref.shape
     heads = logits_w_ref.shape[0]
@@ -290,13 +312,13 @@
                     parts, axis=1
                 ).astype(BF16)
             for t in range(ratio):
-                high_r, low_r = split(right_ref[t, c, 0:rows, :])
+                high_r, low_r = split(right_ref[c * ratio + t, 0:rows, :])
                 lanes = slice(c * k_col, (c + 1) * k_col)
                 r_buf[t * rows : (t + 1) * rows, lanes] = high_r
                 r_buf[cols + t * rows : cols + (t + 1) * rows, lanes] = low_r
         for t in range(ratio):
             mask_buf[:, t * rows : (t + 1) * rows] = (
-                right_ref[t, 0, rows : rows + 8, 0:rows] - 1.0
+                right_ref[t, rows : rows + 8, 0:rows] - 1.0
             ) * 1000000000.0
 
     group = here * seqs
@@ -448,6 +470,7 @@
     ratio = cols // rows
     k_col = factor * seqs
     quarter = rows * seqs // 4
+    half = n_row // 2
     vmem = pl.BlockSpec(memory_space=pltpu.VMEM)
     smem = pl.BlockSpec(memory_space=pltpu.SMEM)
     dma = pltpu.SemaphoreType.DMA
@@ -458,7 +481,7 @@
         functools.partial(exchange_kernel, n_row, n_col, ratio),
         out_shape=(
             jax.ShapeDtypeStruct((n_col,) + left_shape, F32),
-            jax.ShapeDtypeStruct((ratio, n_col) + right_shape, F32),
+            jax.ShapeDtypeStruct((n_row,) + right_shape, F32),
             jax.ShapeDtypeStruct(norm_shape, F32),
         ),
         in_specs=[smem, vmem, vmem, vmem, vmem],
@@ -471,8 +494,11 @@
             pltpu.VMEM(right_shape, F32),
             dma((n_col,)),
             dma((n_col,)),
-            dma((n_row,)),
-            dma((ratio, n_col)),
+            dma((2,)),
+            dma((half,)),
+            dma((half,)),
+            dma((half,)),
+            dma((half,)),
         ],
         compiler_params=pltpu.CompilerParams(
             collective_id=0, has_side_effects=True, vmem_limit_bytes=VMEM_LIMIT
@@ -487,7 +513,6 @@
     )
     here = 8
     steps = rows // here
-    half = n_row // 2
     anywhere = pl.BlockSpec(memory_space=pl.ANY)
     full = lambda shape: pl.BlockSpec(shape, lambda i: (0,) * len(shape), pipeline_mode=pl.Buffered(1))
     pair_out, slots, norm_all = pl.pallas_call(

time: 84.2 us -> 63 us (0.75)
  Pallas kernels: 80.1 us -> 58.9 us
    pallas_call x1, Pallas kernels: 43.7 us -> 22.1 us  [per_device(): pl.pallas_call(functools.partial(exchange_kernel, n_row, n_col, ratio), o...]
where the time goes in v2:
time: 63 us; the launch traced here: 62.8 us
  Pallas kernels  58.9 us (93%)
  local copies, waits for them, and re-layouts  3.22 us (5%)
  between operations  0.65 us (1%)
    pallas_call x1, Pallas kernels, per_device(): pl.pallas_call(functools.partial(pair_kernel, n_row, n_col), grid=(steps,...  29.2 us
    pallas_call x1, Pallas kernels, per_device(): pl.pallas_call(functools.partial(exchange_kernel, n_row, n_col, ratio), o...  22.1 us
    pallas_call x1, Pallas kernels, per_device(): pl.pallas_call(average_kernel, out_shape=jax.ShapeDtypeStruct(alignment.s...  7.57 us
    unnamed x1, local copies, waits for them, and re-layouts  3.22 us

profile of v2, /device:TPU:0, one launch (start us, length us, event | category | flops | bytes accessed | tf_op | source)
XLA Modules:
  0.0 62.8 jit_solution(15520264829726369589)
XLA Ops:
  0.6 22.1 %exchange.1 = (f32[4,104,128]{2,1,0:T(8,128)}, f32[8,56,256]{2,1,0:T(8,128)}, f32[48,512]{1,0:T(8,128)}) custom-call(s32[8]{0:T(128)} %seq_ref.1, s32[1,48]{1,0:T(1,128)} %bitcast.11, f32[8,48,64]{2,1,0:T(8,128)} %align_ref.3, f32[32,64]{1,0:T(8,128)} %bitcast.8, f32[32,64]{1,0:T(8,128)} %bitcast.9), custom_call_target="tpu_custom_call" | custom-call | tf_op jit(solution)/shard_map/exchange/pallas_call | solution.py:480
  22.8 29.2 %pair.1 = (f32[48,96,128]{2,1,0:T(8,128)}, f32[4,384,96]{2,1,0:T(8,128)}, f32[8,48,512]{2,1,0:T(8,128)}) custom-call(f32[4,104,128]{2,1,0:T(8,128)} %get-tuple-element.8.left_ref, f32[8,56,256]{2,1,0:T(8,128)} %get-tuple-element.9.right_ref, f32[1024,128]{1,0:T(8,128)} %outer_ref.1, f32[8,128]{1,0:T(8,128)} %bitcast.10, ...), custom_call_target="tpu_custom_call" | custom-call | tf_op jit(solution)/shard_map/pair/pallas_call | solution.py:518
  52.0 7.6 %average.1 = f32[8,48,64]{2,1,0:T(8,128)} custom-call(f32[4,384,96]{2,1,0:T(8,128)} %get-tuple-element.11.slots, f32[384,512]{1,0:T(8,128)} %bitcast.6, f32[8,48,64]{2,1,0:T(8,128)} %align_ref.3, f32[64,256]{1,0:T(8,128)} %value_w_ref.1, f32[64,256]{1,0:T(8,128)} %gate_w_ref.1, f32[64,256]{1,0:T(8,128)} %bitcast.7), custom_call_target="tpu_custom_call" | custom-call | tf_op jit(solution)/shard_map/average/pallas_call | solution.py:561
  59.6 3.2 %copy.14 = f32[48,96,128]{2,1,0:T(8,128)} copy(f32[48,96,128]{2,1,0:T(8,128)} %get-tuple-element.17) | data formatting | bytes 4718592

commit v3 on v2

--- a/solution.py
+++ b/solution.py
@@ -38,10 +38,11 @@
     return multiply(high, right_high) + (multiply(low, right_high) + multiply(high, right_low))
 
 
-def exchange_kernel(
+def exchange(
     n_row,
     n_col,
     ratio,
+    between,
     seq_ref,
     res_ref,
     align_ref,
@@ -156,6 +157,7 @@
         started.append(copy)
     left_own = pltpu.make_async_copy(left_buf, left_out.at[col], left_recv.at[0])
     left_own.start()
+    between()
     pltpu.make_async_copy(right_buf, right_out.at[row], turn_sem.at[1]).wait()
     for k in range(1, half):
         copy = pltpu.make_async_remote_copy(
@@ -200,11 +202,13 @@
 def pair_kernel(
     n_row,
     n_col,
-    left_ref,
-    right_ref,
+    seq_ref,
+    res_ref,
+    align_ref,
+    left_w_ref,
+    right_w_ref,
     outer_ref,
     logits_w_ref,
-    norm_ref,
     pair_ref,
     pair_out,
     slots,
@@ -224,12 +228,15 @@
     relay_send,
     relay_recv,
     norm_local,
+    left_ref,
+    right_ref,
+    norm_ref,
+    *exchange_scratch,
 ):
     row, col = lax.axis_index("row"), lax.axis_index("col")
     half = n_row // 2
     chip, core = row // 2, lax.rem(row, 2)
     partner = 2 * chip + 1 - core
-    barrier = pltpu.get_barrier_semaphore()
     quarter = left_ref.shape[1] - 8
     ratio, rows = n_row // n_col, right_ref.shape[1] - 8
     k_col = right_ref.shape[2]
@@ -283,20 +290,30 @@
 
     @pl.when(step == 0)
     def _():
-        for k in range(1, n_col):
-            pl.semaphore_signal(
-                barrier, inc=1, device_id=(row, lax.rem(col + k, n_col)), device_id_type=MESH
-            )
-        for k in range(1, half):
-            pl.semaphore_signal(barrier, inc=1, device_id=(peer_row(k), col), device_id_type=MESH)
-        pl.semaphore_signal(barrier, inc=1, device_id=(partner, col), device_id_type=MESH)
+        def between():
+            for b in range(factor):
+                high, low = split(outer_ref[pl.ds(b, factor, stride=factor), :])
+                lanes = slice(b * width, (b + 1) * width)
+                w_buf[0:factor, lanes] = high
+                w_buf[factor : 2 * factor, lanes] = low
+                w_buf[2 * factor : 3 * factor, lanes] = high
+
+        exchange(
+            n_row,
+            n_col,
+            ratio,
+            between,
+            seq_ref,
+            res_ref,
+            align_ref,
+            left_w_ref,
+            right_w_ref,
+            left_ref,
+            right_ref,
+            norm_ref,
+            *exchange_scratch,
+        )
         own_norm.start()
-        for b in range(factor):
-            high, low = split(outer_ref[pl.ds(b, factor, stride=factor), :])
-            lanes = slice(b * width, (b + 1) * width)
-            w_buf[0:factor, lanes] = high
-            w_buf[factor : 2 * factor, lanes] = low
-            w_buf[2 * factor : 3 * factor, lanes] = high
         count = left_ref[0, quarter : quarter + 1, 0:1]
         for c in range(1, n_col):
             count = count + left_ref[c, quarter : quarter + 1, 0:1]
@@ -354,18 +371,20 @@
         sums = first[:cols] + (first[cols:] + dot(r_both[:cols], right_low))
         for t in range(2):
             i = 2 * p + t
-            pair = pair_ref[i] + sums[:, t * width : (t + 1) * width]
-            pair_out[i] = pair
-            high, low = split(layer_norm(pair))
-            one = dot_t(w_both, high)
-            two = dot_t(w_both, low)
+            pair_out[i] = pair_ref[i] + sums[:, t * width : (t + 1) * width]
+    batch = here // 2
+    for g in range(0, here, batch):
+        pairs = pair_out[g : g + batch].reshape(batch * cols, width)
+        high, low = split(layer_norm(pairs))
+        for t in range(batch):
+            one = dot_t(w_both, high[t * cols : (t + 1) * cols])
+            two = dot_t(w_both, low[t * cols : (t + 1) * cols])
             logits = one[:heads] + (one[heads:] + two[:heads])
-            start = pl.multiple_of(step * size + i * heads, heads)
+            start = pl.multiple_of(step * size + (g + t) * heads, heads)
             logits_buf[pl.ds(start, heads), :] = logits + mask_buf[...]
 
     @pl.when(step == 0)
     def _():
-        pl.semaphore_wait(barrier, n_col - 1 + half)
         relay_copy(0).start()
         for k in range(1, half):
             norm_copy(k).start()
@@ -477,40 +496,6 @@
     left_shape = (quarter + 8, 4 * factor)
     right_shape = (rows + 8, k_col)
     norm_shape = (rows, seqs * width)
-    left_all, right_all, norm_own = pl.pallas_call(
-        functools.partial(exchange_kernel, n_row, n_col, ratio),
-        out_shape=(
-            jax.ShapeDtypeStruct((n_col,) + left_shape, F32),
-            jax.ShapeDtypeStruct((n_row,) + right_shape, F32),
-            jax.ShapeDtypeStruct(norm_shape, F32),
-        ),
-        in_specs=[smem, vmem, vmem, vmem, vmem],
-        out_specs=(vmem, vmem, vmem),
-        scratch_shapes=[
-            pltpu.VMEM((rows * seqs, width), F32),
-            pltpu.VMEM(norm_shape, F32),
-            pltpu.VMEM((k_col, seqs * width), F32),
-            pltpu.VMEM(left_shape, F32),
-            pltpu.VMEM(right_shape, F32),
-            dma((n_col,)),
-            dma((n_col,)),
-            dma((2,)),
-            dma((half,)),
-            dma((half,)),
-            dma((half,)),
-            dma((half,)),
-        ],
-        compiler_params=pltpu.CompilerParams(
-            collective_id=0, has_side_effects=True, vmem_limit_bytes=VMEM_LIMIT
-        ),
-        name="exchange",
-    )(
-        seq_mask,
-        res_mask.reshape(1, rows),
-        alignment,
-        left_weight.T,
-        right_weight.T,
-    )
     here = 8
     steps = rows // here
     anywhere = pl.BlockSpec(memory_space=pl.ANY)
@@ -524,11 +509,13 @@
             jax.ShapeDtypeStruct((n_row,) + norm_shape, F32),
         ),
         in_specs=[
-            full(left_all.shape),
-            full(right_all.shape),
+            smem,
+            vmem,
+            vmem,
+            vmem,
+            vmem,
             full(w_outer.shape),
             full((heads, pair_width)),
-            anywhere,
             pl.BlockSpec((here, cols, pair_width), lambda i: (i, 0, 0)),
         ],
         out_specs=(
@@ -552,12 +539,36 @@
             dma((half,)),
             dma((half,)),
             dma,
+            pltpu.VMEM((n_col,) + left_shape, F32),
+            pltpu.VMEM((n_row,) + right_shape, F32),
+            pltpu.VMEM(norm_shape, F32),
+            pltpu.VMEM((rows * seqs, width), F32),
+            pltpu.VMEM(norm_shape, F32),
+            pltpu.VMEM((k_col, seqs * width), F32),
+            pltpu.VMEM(left_shape, F32),
+            pltpu.VMEM(right_shape, F32),
+            dma((n_col,)),
+            dma((n_col,)),
+            dma((2,)),
+            dma((half,)),
+            dma((half,)),
+            dma((half,)),
+            dma((half,)),
         ],
         compiler_params=pltpu.CompilerParams(
-            collective_id=1, has_side_effects=True, vmem_limit_bytes=VMEM_LIMIT
+            collective_id=0, has_side_effects=True, vmem_limit_bytes=VMEM_LIMIT
         ),
         name="pair",
-    )(left_all, right_all, w_outer, w_logits.T, norm_own, pair_rep)
+    )(
+        seq_mask,
+        res_mask.reshape(1, rows),
+        alignment,
+        left_weight.T,
+        right_weight.T,
+        w_outer,
+        w_logits.T,
+        pair_rep,
+    )
     alignment_out = pl.pallas_call(
         average_kernel,
         out_shape=jax.ShapeDtypeStruct(alignment.shape, F32),

time: 63 us -> 53.7 us (0.85)
  Pallas kernels: 58.9 us -> 49.6 us
    pallas_call x1 -> x0, Pallas kernels: 22.1 us -> none  [per_device(): pl.pallas_call(functools.partial(exchange_kernel, n_row, n_col, ratio), o...]
    pallas_call x1, Pallas kernels: 29.2 us -> 42 us  [per_device(): pl.pallas_call(functools.partial(pair_kernel, n_row, n_col), grid=(steps,...]
where the time goes in v3:
time: 53.7 us; the launch traced here: 53.5 us
  Pallas kernels  49.6 us (92%)
  local copies, waits for them, and re-layouts  3.22 us (6%)
  between operations  0.64 us (1%)
    pallas_call x1, Pallas kernels, per_device(): pl.pallas_call(functools.partial(pair_kernel, n_row, n_col), grid=(steps,...  42 us
    pallas_call x1, Pallas kernels, per_device(): pl.pallas_call(average_kernel, out_shape=jax.ShapeDtypeStruct(alignment.s...  7.57 us
    unnamed x1, local copies, waits for them, and re-layouts  3.22 us

profile of v3, /device:TPU:0, one launch (start us, length us, event | category | flops | bytes accessed | tf_op | source)
XLA Modules:
  0.0 53.5 jit_solution(83253423660380284)
XLA Ops:
  0.6 42.0 %pair.1 = (f32[48,96,128]{2,1,0:T(8,128)}, f32[4,384,96]{2,1,0:T(8,128)}, f32[8,48,512]{2,1,0:T(8,128)}) custom-call(s32[8]{0:T(128)} %seq_ref.1, s32[1,48]{1,0:T(1,128)} %bitcast.11, f32[8,48,64]{2,1,0:T(8,128)} %align_ref.3, f32[32,64]{1,0:T(8,128)} %bitcast.8, f32[32,64]{1,0:T(8,128)} %bitcast.9, f32[1024,128]{1,0:T(8,128)} %outer_ref.1, ...), custom_call_target="tpu_custom_call" | custom-call | tf_op jit(solution)/shard_map/pair/pallas_call | solution.py:503
  42.7 7.6 %average.1 = f32[8,48,64]{2,1,0:T(8,128)} custom-call(f32[4,384,96]{2,1,0:T(8,128)} %get-tuple-element.5.slots, f32[384,512]{1,0:T(8,128)} %bitcast.6, f32[8,48,64]{2,1,0:T(8,128)} %align_ref.3, f32[64,256]{1,0:T(8,128)} %value_w_ref.1, f32[64,256]{1,0:T(8,128)} %gate_w_ref.1, f32[64,256]{1,0:T(8,128)} %bitcast.7), custom_call_target="tpu_custom_call" | custom-call | tf_op jit(solution)/shard_map/average/pallas_call | solution.py:572
  50.2 3.2 %copy.14 = f32[48,96,128]{2,1,0:T(8,128)} copy(f32[48,96,128]{2,1,0:T(8,128)} %get-tuple-element.11) | data formatting | bytes 4718592

commit v4 on v3

--- a/solution.py
+++ b/solution.py
@@ -430,9 +430,15 @@
     value_w_ref,
     gate_w_ref,
     output_w_ref,
+    pair_ref,
     out_ref,
+    pair_out,
     terms_buf,
+    pair_buf,
+    pair_sem,
 ):
+    bring = pltpu.make_async_copy(pair_ref, pair_buf, pair_sem.at[0])
+    bring.start()
     seqs, rows, width = align_ref.shape
     n_col, total_rows, cols = slots.shape
     heads = total_rows // rows
@@ -459,12 +465,16 @@
         high, low = split(norm_ref[c * cols : (c + 1) * cols, :])
         part = dot_split(terms_buf[c] * inverse, high, low)
         mixed = part if mixed is None else mixed + part
+    bring.wait()
+    place = pltpu.make_async_copy(pair_buf, pair_out, pair_sem.at[1])
+    place.start()
     for s in range(seqs):
         wide = dot_split(mixed[:, s * width : (s + 1) * width], wv_high, wv_low)
         averaged = jnp.sum(wide.reshape(rows, heads, channels) * own_head[None], axis=1)
         align = align_ref[s]
         gate = jax.nn.sigmoid(dot_split(layer_norm(align), wg_high, wg_low))
         out_ref[s] = align + dot_split(gate * averaged, wo_high, wo_low, dot_t)
+    place.wait()
 
 
 def per_device(
@@ -569,12 +579,19 @@
         w_logits.T,
         pair_rep,
     )
-    alignment_out = pl.pallas_call(
+    alignment_out, pair_final = pl.pallas_call(
         average_kernel,
-        out_shape=jax.ShapeDtypeStruct(alignment.shape, F32),
-        in_specs=[vmem] * 6,
-        out_specs=vmem,
-        scratch_shapes=[pltpu.VMEM(slots.shape, F32)],
+        out_shape=(
+            jax.ShapeDtypeStruct(alignment.shape, F32),
+            jax.ShapeDtypeStruct(pair_rep.shape, F32),
+        ),
+        in_specs=[vmem] * 6 + [anywhere],
+        out_specs=(vmem, anywhere),
+        scratch_shapes=[
+            pltpu.VMEM(slots.shape, F32),
+            pltpu.VMEM(pair_rep.shape, F32),
+            dma((2,)),
+        ],
         compiler_params=pltpu.CompilerParams(vmem_limit_bytes=VMEM_LIMIT),
         name="average",
     )(
@@ -584,8 +601,9 @@
         value_weight,
         gate_weight,
         output_weight.T,
+        pair_out,
     )
-    return (alignment_out, pair_out)
+    return (alignment_out, pair_final)
 
 
 def solution(mesh):

time: 53.7 us -> 50.6 us (0.942)
  local copies, waits for them, and re-layouts: 3.22 us -> 0 us
    unnamed x1 -> x0, local copies, waits for them, and re-layouts: 3.22 us -> none
where the time goes in v4:
time: 50.6 us; the launch traced here: 50.4 us
  Pallas kernels  49.8 us (98%)
  between operations  0.64 us (1%)
    pallas_call x1, Pallas kernels, per_device(): pl.pallas_call(functools.partial(pair_kernel, n_row, n_col), grid=(steps,...  42 us
    pallas_call x1, Pallas kernels, per_device(): pl.pallas_call(average_kernel, out_shape=(jax.ShapeDtypeStruct(alignment....  7.74 us

profile of v4, /device:TPU:0, one launch (start us, length us, event | category | flops | bytes accessed | tf_op | source)
XLA Modules:
  0.0 50.4 jit_solution(17031582840984384055)
XLA Ops:
  0.6 42.0 %pair.1 = (f32[48,96,128]{2,1,0:T(8,128)}, f32[4,384,96]{2,1,0:T(8,128)}, f32[8,48,512]{2,1,0:T(8,128)}) custom-call(s32[8]{0:T(128)} %seq_ref.1, s32[1,48]{1,0:T(1,128)} %bitcast.11, f32[8,48,64]{2,1,0:T(8,128)} %align_ref.3, f32[32,64]{1,0:T(8,128)} %bitcast.8, f32[32,64]{1,0:T(8,128)} %bitcast.9, f32[1024,128]{1,0:T(8,128)} %outer_ref.1, ...), custom_call_target="tpu_custom_call" | custom-call | tf_op jit(solution)/shard_map/pair/pallas_call | solution.py:513
  42.7 7.7 %average.1 = (f32[8,48,64]{2,1,0:T(8,128)}, f32[48,96,128]{2,1,0:T(8,128)}) custom-call(f32[4,384,96]{2,1,0:T(8,128)} %get-tuple-element.5.slots, f32[384,512]{1,0:T(8,128)} %bitcast.6, f32[8,48,64]{2,1,0:T(8,128)} %align_ref.3, f32[64,256]{1,0:T(8,128)} %value_w_ref.1, f32[64,256]{1,0:T(8,128)} %gate_w_ref.1, f32[64,256]{1,0:T(8,128)} %bitcast.7, ...), custom_call_target="tpu_custom_call" | custom-call | tf_op jit(solution)/shard_map/average/pallas_call | solution.py:582
